TPU v7x, 256 devices: a whole 4x4x8 slice. The times are simulated.
256 devices in a mesh: blk: 16 (over x_lo, y, core), rows: 16 (over x_hi, z).
Axes of the slice: x: 4 (x_hi: 2, x_lo: 2; x = x_hi * 2 + x_lo), y: 4, z: 8, core: 2. Of those that a mesh axis runs over, the one named last changes fastest.
Arguments:
- excitations: float32 [64, 131072], P(None, ('blk', 'rows')), may hold values from -6 to 6
- adjoint_loads: float32 [64, 131072], P(None, ('blk', 'rows')), may hold values from -6 to 6
- near_tiles: bfloat16 [8192, 256, 256], P(('blk', 'rows')), may hold values from -0.125 to 0.125
- tile_rows: int32 [8192], P(('blk', 'rows')), may hold values from 0 to 1
- tile_cols: int32 [8192], P(('blk', 'rows')), may hold values from 0 to 31
- tile_count: int32 [256], P(('blk', 'rows')), may hold values from 4 to 32, as said below
- skeleton_in: bfloat16 [1024, 131072], P(None, ('blk', 'rows')), may hold values from -0.0625 to 0.0625
- skeleton_out: bfloat16 [1024, 131072], P(None, ('blk', 'rows')), may hold values from -0.1875 to 0.1875
- translation: float32 [16, 15, 1024, 1024], P('blk', None, 'rows'), may hold values from -0.046875 to 0.046875
Outputs:
- response: float32 [64, 131072], P(None, ('blk', 'rows'))
- sensitivity: float32 [64, 131072], P(None, ('blk', 'rows'))
Inputs may be any that keep to these rules, and one draw needn't show every extreme that they name: `tile_count`: slots of a device are used from slot 0 on; later slots are no part of the operator.
All inputs are finite; a program needn't handle non-finite values.
Results may differ from a plain program's by a relative error of at most 0.0036.
Values may be sent and summed in bfloat16 or wider, within the bound.
No kernel may reach another device: no remote copies, remote signals or barrier semaphores. Data moves between devices by JAX's collectives and lax.ppermute only.
A program may use at most 128 MiB of HBM per device.

v0:
```python
import jax
import jax.numpy as jnp
from jax import lax
from jax.sharding import PartitionSpec as P

highest = lax.Precision.HIGHEST


def on_device(
    excitations,
    adjoint_loads,
    near_tiles,
    tile_rows,
    tile_cols,
    tile_count,
    skeleton_in,
    skeleton_out,
    translation,
):
    drive_low = excitations.astype(jnp.bfloat16)
    loads_low = adjoint_loads.astype(jnp.bfloat16)
    excite_count = excitations.shape[0]
    panels = excitations.shape[1]
    tile_size = near_tiles.shape[1]
    kernels = translation[0]
    share_width = kernels.shape[1]
    clusters = lax.axis_size("blk")
    cluster = lax.axis_index("blk")
    gathered = lax.all_gather(drive_low, "rows", axis=1, tiled=True)
    column_blocks = gathered.shape[1] // tile_size
    row_blocks = panels // tile_size
    drive_blocks = gathered.reshape(excite_count, column_blocks, tile_size)
    load_blocks = loads_low.reshape(excite_count, row_blocks, tile_size)
    used_slots = tile_count[0]

    def near_group(group_index, carry):
        ahead, behind = carry
        first_slot = group_index * 4
        tile_group = lax.dynamic_slice_in_dim(near_tiles, first_slot, 4, 0)
        row_ids = lax.dynamic_slice_in_dim(tile_rows, first_slot, 4, 0)
        column_ids = lax.dynamic_slice_in_dim(tile_cols, first_slot, 4, 0)
        live_mask = (first_slot + jnp.arange(4, dtype=jnp.int32) < used_slots).astype(jnp.float32)[
            None, :, None
        ]
        source = jnp.take(drive_blocks, column_ids, axis=1)
        target = jnp.take(load_blocks, row_ids, axis=1)
        forward = (
            jnp.einsum("egj,gij->egi", source, tile_group, preferred_element_type=jnp.float32)
            * live_mask
        )
        backward = (
            jnp.einsum("egi,gij->egj", target, tile_group, preferred_element_type=jnp.float32)
            * live_mask
        )
        return (ahead.at[:, row_ids].add(forward), behind.at[:, column_ids].add(backward))

    near_start = (
        jnp.zeros((excite_count, row_blocks, tile_size), jnp.float32),
        jnp.zeros((excite_count, column_blocks, tile_size), jnp.float32),
    )
    near_ahead, near_behind = lax.fori_loop(0, (used_slots + 3) // 4, near_group, near_start)
    contract_panels = (((1,), (1,)), ((), ()))
    charge_part = lax.dot_general(
        drive_low, skeleton_in, contract_panels, preferred_element_type=jnp.float32
    )
    gradient_part = lax.dot_general(
        loads_low, skeleton_out, contract_panels, preferred_element_type=jnp.float32
    )
    charges, gradient_all = lax.psum((charge_part, gradient_part), "rows")
    gradient = lax.dynamic_slice_in_dim(
        gradient_all, lax.axis_index("rows") * share_width, share_width, 1
    )

    def offsets_for(other_ids):
        offset = jnp.remainder(cluster - other_ids, clusters)
        active = (offset != 0).astype(jnp.float32)
        return (jnp.maximum(offset - 1, 0), active)

    charge_piece = lax.all_gather(charges[None], "blk", axis=0, tiled=True)
    span_count = charge_piece.shape[0]
    offset, active = offsets_for(jnp.arange(span_count, dtype=jnp.int32))
    chosen = jnp.take(kernels, offset, axis=0)
    potential = jnp.einsum(
        "cej,ckj->ek", charge_piece * active[:, None, None], chosen, precision=highest
    )
    potential_low = lax.all_gather(potential.astype(jnp.bfloat16), "rows", axis=1, tiled=True)
    far_ahead = jnp.dot(potential_low, skeleton_out, preferred_element_type=jnp.float32)
    offset, active = offsets_for(jnp.arange(lax.axis_size("blk") * 1, dtype=jnp.int32))
    chosen = jnp.take(kernels, offset, axis=0)
    summed = lax.psum_scatter(
        jnp.einsum("ek,ckj->cej", gradient, chosen, precision=highest) * active[:, None, None],
        "blk",
        scatter_dimension=0,
        tiled=True,
    )
    adjoint_low = lax.psum(summed[0], "rows").astype(jnp.bfloat16)
    far_behind = jnp.dot(adjoint_low, skeleton_in, preferred_element_type=jnp.float32)
    near_columns = lax.psum_scatter(
        near_behind.reshape(excite_count, column_blocks * tile_size),
        "rows",
        scatter_dimension=1,
        tiled=True,
    )
    response = near_ahead.reshape(excite_count, panels) + far_ahead
    sensitivity = near_columns + far_behind
    return (response, sensitivity)


def solution(mesh):
    return jax.shard_map(
        on_device,
        mesh=mesh,
        in_specs=(
            P(None, ("blk", "rows")),
            P(None, ("blk", "rows")),
            P(("blk", "rows"), None, None),
            P(("blk", "rows")),
            P(("blk", "rows")),
            P(("blk", "rows")),
            P(None, ("blk", "rows")),
            P(None, ("blk", "rows")),
            P("blk", None, "rows", None),
        ),
        out_specs=(P(None, ("blk", "rows")), P(None, ("blk", "rows"))),
        check_vma=False,
    )
```

profile of v0, /device:TPU:8, one launch (start us, length us, event | category | flops | bytes accessed | tf_op | source)
XLA Modules:
  0.0 574.7 jit_solution(14490784234258708478)
XLA Ops:
  7.2 1.0 convert_element_type.27
  8.2 0.9 convert_element_type.28
  9.2 2.4 convolution_bitcast_fusion
  11.6 1.1 fusion.45
  13.5 159.0 %all-reduce.4.cloned.1.call-done = (f32[1,64,1024]{2,1,0:T(8,128)}, f32[64,1024]{1,0:T(8,128)}) async-done(((f32[1,64,1024]{2,1,0:T(8,128)}, f32[64,1024]{1,0:T(8,128)}), (f32[1,64,1024]{2,1,0:T(8,128)}, f32[64,1024]{1,0:T(8,128)})) %all-reduce.4.cloned.1.call-update) | async-done | bytes 524304 | tf_op jit(solution)/shard_map/psum | solution.py:69
  172.6 4.9 gather_fusion.2
  178.1 10.0 %multiply_bitcast_fusion = f32[16,64,1024]{2,1,0:T(8,128)} fusion(f32[16,64,1024]{2,1,0:T(8,128)} %gather_fusion.2, f32[16]{0:T(128)S(1)} %get-tuple-element.106, pred[16]{0:T(512)(128)(4,1)S(1)} %get-tuple-element.107, f32[64,1024]{1,0:T(8,128)} %get-tuple-element.100, s32[]{:T(128)S(6)} %select_n.53), kind=kOutput, calls=%fused_computation.30 | convolution fusion | flops 807403520 | bytes 8421460 | tf_op jit(solution)/shard_map/ek,ckj->cej/dot_general | solution.py:91
  189.5 59.3 %all-gather.3.cloned.1.call-done = bf16[64,8192]{1,0:T(8,128)(2,1)} async-done(((bf16[64,512]{1,0:T(8,128)(2,1)}), bf16[64,8192]{1,0:T(8,128)(2,1)}) %all-gather.3.cloned.1.call-update) | async-done | bytes 1048592 | tf_op jit(solution)/shard_map/all_gather | solution.py:29
  248.8 2.3 copy.32
  251.4 65.4 %while.12 = (s32[]{:T(128)}, f32[64,2,256]{2,0,1:T(8,128)S(1)}, f32[64,32,256]{2,0,1:T(8,128)S(1)}, s32[]{:T(128)}, s32[32]{0:T(128)}, /*index=5*/bf16[32,256,25...) while((s32[]{:T(128)}, f32[64,2,256]{2,0,1:T(8,128)S(1)}, ...), condition=%wide.region_3.4_spmd, body=%wide.region_0.3_spmd.sunk | while | flops 67504192 | bytes 3940779 | solution.py:61
  251.4 1.4 compare_and_fusion.4
  252.8 2.0 gather_fusion.1
  254.9 1.4 fusion.65
  256.2 0.7 compare_and_fusion.5
  257.0 0.8 scatter_fusion.1
  257.7 2.4 gather_fusion
  260.2 1.3 fusion.64
  261.5 0.7 scatter_fusion
  262.3 1.4 compare_and_fusion.4
  263.7 2.1 gather_fusion.1
  265.7 1.4 fusion.65
  267.1 0.7 compare_and_fusion.5
  267.9 0.8 scatter_fusion.1
  268.6 2.4 gather_fusion
  271.1 1.4 fusion.64
  272.4 0.7 scatter_fusion
  273.2 1.4 compare_and_fusion.4
  274.6 2.1 gather_fusion.1
  276.7 1.4 fusion.65
  278.0 0.7 compare_and_fusion.5
  278.8 0.8 scatter_fusion.1
  279.6 2.4 gather_fusion
  282.0 1.4 fusion.64
  283.4 0.7 scatter_fusion
  284.1 1.4 compare_and_fusion.4
  285.5 2.0 gather_fusion.1
  287.6 1.4 fusion.65
  288.9 0.7 compare_and_fusion.5
  289.7 0.8 scatter_fusion.1
  290.5 2.4 gather_fusion
  292.9 1.3 fusion.64
  294.2 0.7 scatter_fusion
  295.0 1.4 compare_and_fusion.4
  296.4 2.0 gather_fusion.1
  298.5 1.4 fusion.65
  300.6 0.7 scatter_fusion.1
  301.3 2.4 gather_fusion
  303.8 1.4 fusion.64
  305.1 0.7 scatter_fusion
  305.9 1.4 compare_and_fusion.4
  307.3 2.1 gather_fusion.1
  309.4 1.4 fusion.65
  310.7 0.7 compare_and_fusion.5
  311.5 0.7 scatter_fusion.1
  312.3 2.5 gather_fusion
  314.7 1.3 fusion.64
  316.1 0.8 scatter_fusion
  316.8 1.5 copy.29
  318.5 7.5 %fusion.33 = bf16[64,64]{1,0:T(8,128)(2,1)S(1)} fusion(f32[16,64,1024]{2,1,0:T(8,128)} %gather_fusion.2, pred[16]{0:T(512)(128)(4,1)S(1)} %copy-done.6, f32[16,64,1024]{2,1,0:T(8,128)} %all-gather.5.cloned.1.call-done, f32[16]{0:T(128)S(1)} %copy-done.4), kind=kOutput, calls=%fused_computation.45 | convolution fusion | flops 807407616 | bytes 8396880 | tf_op jit(solution)/shard_map/cej,ckj->ek/dot_general | solution.py:83
  326.0 49.2 %all_gather.11 = bf16[64,1024]{0,1:T(8,128)(2,1)S(1)} all-gather(bf16[64,64]{0,1:T(8,128)(2,1)S(1)} %copy.24), channel_id=1, replica_groups=mesh['blk'=16,'rows'=16] {'rows'}, dimensions={1}, use_global_device_ids=true | all-gather | bytes 139264 | tf_op jit(solution)/shard_map/all_gather | solution.py:86
  375.2 1.0 convolution_add_fusion.1
  376.2 75.2 %all-reduce.5 = bf16[64,1024]{1,0:T(8,128)(2,1)S(1)} all-reduce(f32[64,1024]{1,0:T(8,128)} %bitcast.61), channel_id=1, replica_groups=mesh['blk'=16,'rows'=16] {'rows'}, use_global_device_ids=true, to_apply=%region_8.10 | all-reduce | flops 65536 | bytes 393216 | tf_op jit(solution)/shard_map/psum | solution.py:96
  451.5 114.8 %reduce-scatter.3.cloned.1.call-done = f32[64,512]{1,0:T(8,128)} async-done(((f32[64,8192]{1,0:T(8,128)}), f32[64,512]{1,0:T(8,128)}) %reduce-scatter.3.cloned.1.call-update) | async-done | bytes 131088 | tf_op jit(solution)/shard_map/reduce_scatter | solution.py:98
  566.3 1.9 convolution_add_fusion
  (47 shorter events, 3.4 us)
Async XLA Ops:
  7.2 4.4 copy-start
  7.2 165.3 %all-reduce.4.cloned.1.call-start = ((), (), s32[]{:S(2)}) async-start(), calls=%async_computation.6 | async-start | bytes 1048576 | tf_op jit(solution)/shard_map/psum | solution.py:69
  8.2 4.6 copy-start.2
  12.7 236.1 %all-gather.3.cloned.1.call-start = ((), (), s32[]{:S(2)}) async-start(), calls=%async_computation.2 | async-start | bytes 1114112 | tf_op jit(solution)/shard_map/all_gather | solution.py:29
  13.5 305.0 %all-gather.5.cloned.1.call-start = ((), (), s32[]{:S(2)}) async-start(), calls=%async_computation.3 | async-start | bytes 4456448 | tf_op jit(solution)/shard_map/all_gather | solution.py:79
  172.5 203.7 %reduce-scatter.5.cloned.1.call-start = ((), (), s32[]{:S(2)}) async-start(), calls=%async_computation.5 | async-start | bytes 4456448 | tf_op jit(solution)/shard_map/reduce_scatter | solution.py:90
  177.5 0.5 copy-start.3
  177.5 0.6 copy-start.5
  188.2 378.1 %reduce-scatter.3.cloned.1.call-start = ((), (), s32[]{:S(2)}) async-start(), calls=%async_computation.4 | async-start | bytes 2228224 | tf_op jit(solution)/shard_map/reduce_scatter | solution.py:98
  316.8 1.6 copy-start.4
  316.8 1.6 copy-start.6
  318.4 247.8 %copy-start.1 = (bf16[1024,512]{1,0:T(8,128)(2,1)S(1)}, bf16[1024,512]{1,0:T(8,128)(2,1)}, u32[]{:S(2)}) copy-start(bf16[1024,512]{1,0:T(8,128)(2,1)} %param.19) | copy-start | bytes 3145732
Sparse Core Ops, SparseCore 0:
  12.9 159.5 all-reduce.3
  175.9 72.9 all-gather.2
  250.8 35.9 all-gather.4
  289.4 65.9 reduce-scatter.4
  359.6 206.6 reduce-scatter.2
where the time goes:
time: 576 us; the launch traced here: 575 us
  waiting for transfers between devices  334 us (58%)
  blocking collectives  124 us (22%)
  matrix products  40.2 us (7%)
  local copies, waits for them, and re-layouts  37.3 us (6%)
  other arithmetic  23.8 us (4%)
  between operations  14.6 us (3%)
    psum x1, waiting for transfers between devices, on_device(): charges, gradient_all = lax.psum((charge_part, gradient_part), 'rows')  159 us
    reduce_scatter x1, waiting for transfers between devices, on_device(): lax.psum_scatter(near_behind.reshape(excite_count, column_blocks * tile_s...  115 us
    psum x1, blocking collectives, on_device(): adjoint_low = lax.psum(summed[0], 'rows').astype(jnp.bfloat16)  75.2 us
    all_gather x1, waiting for transfers between devices, on_device(): gathered = lax.all_gather(drive_low, 'rows', axis=1, tiled=True)  59.3 us
    all_gather x1, blocking collectives, on_device(): lax.all_gather(potential.astype(jnp.bfloat16), 'rows', axis=1, tiled=True)  49.2 us
    gather x6, local copies, waits for them, and re-layouts, near_group(): source = jnp.take(drive_blocks, column_ids, axis=1)  14.6 us
    gather x6, local copies, waits for them, and re-layouts, near_group(): target = jnp.take(load_blocks, row_ids, axis=1)  12.3 us
  transfers between devices with their start and end apart: 5, of which 3 were waited for; matrix products, arithmetic and copies ran while one was open for 16% of the time, Pallas kernels for 0%

commit v1 on v0

--- a/solution.py
+++ b/solution.py
@@ -93,7 +93,7 @@
         scatter_dimension=0,
         tiled=True,
     )
-    adjoint_low = lax.psum(summed[0], "rows").astype(jnp.bfloat16)
+    adjoint_low = jnp.sum(lax.all_gather(summed[0], "rows"), axis=0).astype(jnp.bfloat16)
     far_behind = jnp.dot(adjoint_low, skeleton_in, preferred_element_type=jnp.float32)
     near_columns = lax.psum_scatter(
         near_behind.reshape(excite_count, column_blocks * tile_size),

time: 576 us -> 685 us (1.19)
  waiting for transfers between devices: 334 us -> 514 us
  blocking collectives: 124 us -> 49.8 us
    reduce_scatter x1, waiting for transfers between devices: 115 us -> 203 us  [on_device(): lax.psum_scatter(near_behind.reshape(excite_count, column_blocks * tile_s...]
    psum x1 -> x0, blocking collectives: 75.2 us -> none  [on_device(): adjoint_low = lax.psum(summed[0], 'rows').astype(jnp.bfloat16)]
    reduce_scatter x1, waiting for transfers between devices: 0.01 us -> 61.5 us  [on_device(): lax.psum_scatter(jnp.einsum('ek,ckj->cej', gradient, chosen, precision=hi...]
    all_gather x1, waiting for transfers between devices: 59.3 us -> 80.2 us  [on_device(): gathered = lax.all_gather(drive_low, 'rows', axis=1, tiled=True)]
    all_gather x0 -> x1, waiting for transfers between devices: none -> 14.2 us  [on_device(): lax.all_gather(summed[0], 'rows')]
  transfers between devices with their start and end apart: 5 -> 6, of which waited for: 3 -> 5; matrix products, arithmetic and copies ran while one was open for 16% -> 13% of each run, Pallas kernels for 0% -> 0%
where the time goes in v1:
time: 685 us; the launch traced here: 683 us
  waiting for transfers between devices  514 us (75%)
  blocking collectives  49.8 us (7%)
  matrix products  40 us (6%)
  local copies, waits for them, and re-layouts  36.9 us (5%)
  other arithmetic  26.3 us (4%)
  between operations  14.9 us (2%)
    reduce_scatter x1, waiting for transfers between devices, on_device(): lax.psum_scatter(near_behind.reshape(excite_count, column_blocks * tile_s...  203 us
    psum x1, waiting for transfers between devices, on_device(): charges, gradient_all = lax.psum((charge_part, gradient_part), 'rows')  155 us
    all_gather x1, waiting for transfers between devices, on_device(): gathered = lax.all_gather(drive_low, 'rows', axis=1, tiled=True)  80.2 us
    reduce_scatter x1, waiting for transfers between devices, on_device(): lax.psum_scatter(jnp.einsum('ek,ckj->cej', gradient, chosen, precision=hi...  61.5 us
    all_gather x1, blocking collectives, on_device(): lax.all_gather(potential.astype(jnp.bfloat16), 'rows', axis=1, tiled=True)  49.8 us
    gather x6, local copies, waits for them, and re-layouts, near_group(): source = jnp.take(drive_blocks, column_ids, axis=1)  14.8 us
    all_gather x1, waiting for transfers between devices, on_device(): lax.all_gather(summed[0], 'rows')  14.2 us
  transfers between devices with their start and end apart: 6, of which 5 were waited for; matrix products, arithmetic and copies ran while one was open for 13% of the time, Pallas kernels for 0%

profile of v1, /device:TPU:8, one launch (start us, length us, event | category | flops | bytes accessed | tf_op | source)
XLA Modules:
  0.0 683.0 jit_solution(902637576204597549)
XLA Ops:
  7.2 1.0 convert_element_type.27
  8.2 0.9 convert_element_type.28
  9.2 2.4 convolution_bitcast_fusion
  11.6 1.1 fusion.45
  12.8 4.9 gather_fusion.2
  17.7 154.8 %all-reduce.3.cloned.1.call-done = (f32[1,64,1024]{2,1,0:T(8,128)}, f32[64,1024]{1,0:T(8,128)}) async-done(((f32[1,64,1024]{2,1,0:T(8,128)}, f32[64,1024]{1,0:T(8,128)}), (f32[1,64,1024]{2,1,0:T(8,128)}, f32[64,1024]{1,0:T(8,128)})) %all-reduce.3.cloned.1.call-update) | async-done | bytes 524304 | tf_op jit(solution)/shard_map/psum | solution.py:69
  172.5 10.0 %multiply_bitcast_fusion = f32[16,64,1024]{2,1,0:T(8,128)} fusion(f32[16,64,1024]{2,1,0:T(8,128)} %gather_fusion.2, f32[16]{0:T(128)S(1)} %get-tuple-element.106, pred[16]{0:T(512)(128)(4,1)S(1)} %get-tuple-element.107, f32[64,1024]{1,0:T(8,128)} %get-tuple-element.100, s32[]{:T(128)S(6)} %select_n.53), kind=kOutput, calls=%fused_computation.30 | convolution fusion | flops 807403520 | bytes 8421460 | tf_op jit(solution)/shard_map/ek,ckj->cej/dot_general | solution.py:91
  183.9 61.5 %reduce-scatter.5.cloned.1.call-done = f32[1,64,1024]{2,1,0:T(8,128)} async-done(((f32[16,64,1024]{2,1,0:T(8,128)}), f32[1,64,1024]{2,1,0:T(8,128)}) %reduce-scatter.5.cloned.1.call-update) | async-done | bytes 262160 | tf_op jit(solution)/shard_map/reduce_scatter | solution.py:90
  246.8 80.2 %all-gather.4.cloned.1.call-done = bf16[64,8192]{1,0:T(8,128)(2,1)} async-done(((bf16[64,512]{1,0:T(8,128)(2,1)}), bf16[64,8192]{1,0:T(8,128)(2,1)}) %all-gather.4.cloned.1.call-update) | async-done | bytes 1048592 | tf_op jit(solution)/shard_map/all_gather | solution.py:29
  327.0 2.4 copy.32
  329.7 65.5 %while.12 = (s32[]{:T(128)}, f32[64,2,256]{2,0,1:T(8,128)S(1)}, f32[64,32,256]{2,0,1:T(8,128)S(1)}, s32[]{:T(128)}, s32[32]{0:T(128)}, /*index=5*/bf16[32,256,25...) while((s32[]{:T(128)}, f32[64,2,256]{2,0,1:T(8,128)S(1)}, ...), condition=%wide.region_3.4_spmd, body=%wide.region_0.3_spmd.sunk | while | flops 67504192 | bytes 3940779 | solution.py:61
  329.7 1.4 compare_and_fusion.4
  331.1 2.0 gather_fusion.1
  333.1 1.4 fusion.65
  334.5 0.7 compare_and_fusion.5
  335.2 0.8 scatter_fusion.1
  336.0 2.5 gather_fusion
  338.6 1.3 fusion.64
  339.9 0.7 scatter_fusion
  340.7 1.4 compare_and_fusion.4
  342.1 2.1 gather_fusion.1
  344.1 1.4 fusion.65
  345.5 0.7 compare_and_fusion.5
  346.3 0.8 scatter_fusion.1
  347.0 2.4 gather_fusion
  349.5 1.3 fusion.64
  350.8 0.7 scatter_fusion
  351.6 1.4 compare_and_fusion.4
  353.0 2.0 gather_fusion.1
  355.0 1.4 fusion.65
  356.4 0.7 compare_and_fusion.5
  357.2 0.8 scatter_fusion.1
  357.9 2.5 gather_fusion
  360.4 1.3 fusion.64
  361.8 0.7 scatter_fusion
  362.5 1.4 compare_and_fusion.4
  363.9 2.0 gather_fusion.1
  366.0 1.4 fusion.65
  368.1 0.8 scatter_fusion.1
  368.9 2.4 gather_fusion
  371.3 1.3 fusion.64
  372.6 0.7 scatter_fusion
  373.4 1.4 compare_and_fusion.4
  374.8 2.0 gather_fusion.1
  376.9 1.4 fusion.65
  379.0 0.7 scatter_fusion.1
  379.7 2.5 gather_fusion
  382.2 1.3 fusion.64
  383.6 0.7 scatter_fusion
  384.3 1.4 compare_and_fusion.4
  385.7 2.0 gather_fusion.1
  387.8 1.4 fusion.65
  389.9 0.7 scatter_fusion.1
  390.7 2.4 gather_fusion
  393.1 1.3 fusion.64
  394.4 0.7 scatter_fusion
  395.2 1.5 copy.29
  396.9 7.3 %fusion.33 = bf16[64,64]{1,0:T(8,128)(2,1)S(1)} fusion(f32[16,64,1024]{2,1,0:T(8,128)} %gather_fusion.2, pred[16]{0:T(512)(128)(4,1)S(1)} %copy-done.6, f32[16,64,1024]{2,1,0:T(8,128)} %all-gather.6.cloned.1.call-done, f32[16]{0:T(128)S(1)} %copy-done.4), kind=kOutput, calls=%fused_computation.45 | convolution fusion | flops 807407616 | bytes 8396880 | tf_op jit(solution)/shard_map/cej,ckj->ek/dot_general | solution.py:83
  404.3 49.8 %all_gather.14 = bf16[64,1024]{0,1:T(8,128)(2,1)S(1)} all-gather(bf16[64,64]{0,1:T(8,128)(2,1)S(1)} %copy.24), channel_id=1, replica_groups=mesh['blk'=16,'rows'=16] {'rows'}, dimensions={1}, use_global_device_ids=true | all-gather | bytes 139264 | tf_op jit(solution)/shard_map/all_gather | solution.py:86
  454.1 1.0 convolution_add_fusion.1
  455.1 14.2 %all-gather.8.cloned.1.call-done = f32[16,64,1024]{2,1,0:T(8,128)} async-done(((f32[1,64,1024]{2,1,0:T(8,128)}), f32[16,64,1024]{2,1,0:T(8,128)}) %all-gather.8.cloned.1.call-update) | async-done | bytes 4194320 | tf_op jit(solution)/shard_map/all_gather | solution.py:96
  469.3 2.5 reduce_sum.9
  471.8 202.5 %reduce-scatter.3.cloned.1.call-done = f32[64,512]{1,0:T(8,128)} async-done(((f32[64,8192]{1,0:T(8,128)}), f32[64,512]{1,0:T(8,128)}) %reduce-scatter.3.cloned.1.call-update) | async-done | bytes 131088 | tf_op jit(solution)/shard_map/reduce_scatter | solution.py:98
  674.3 1.9 convolution_add_fusion
  (50 shorter events, 4.9 us)
Async XLA Ops:
  7.2 4.4 copy-start
  7.2 165.3 %all-reduce.3.cloned.1.call-start = ((), (), s32[]{:S(2)}) async-start(), calls=%async_computation.7 | async-start | bytes 1048576 | tf_op jit(solution)/shard_map/psum | solution.py:69
  8.2 9.5 %copy-start.2 = (bf16[64,512]{1,0:T(8,128)(2,1)}, bf16[64,512]{1,0:T(8,128)(2,1)S(1)}, u32[]{:S(2)}) copy-start(bf16[64,512]{1,0:T(8,128)(2,1)S(1)} %convert_element_type.27) | copy-start | bytes 196612
  12.7 232.7 %reduce-scatter.5.cloned.1.call-start = ((), (), s32[]{:S(2)}) async-start(), calls=%async_computation.5 | async-start | bytes 4456448 | tf_op jit(solution)/shard_map/reduce_scatter | solution.py:90
  17.7 164.8 %copy-start.3 = (f32[16]{0:T(128)}, f32[16]{0:T(128)S(1)}, u32[]{:S(2)}) copy-start(f32[16]{0:T(128)S(1)} %get-tuple-element.106) | copy-start | bytes 196
  17.7 164.8 %copy-start.5 = (pred[16]{0:T(512)(128)(4,1)}, pred[16]{0:T(512)(128)(4,1)S(1)}, u32[]{:S(2)}) copy-start(pred[16]{0:T(512)(128)(4,1)S(1)} %get-tuple-element.107) | copy-start | bytes 52
  182.6 144.4 %all-gather.4.cloned.1.call-start = ((), (), s32[]{:S(2)}) async-start(), calls=%async_computation.2 | async-start | bytes 1114112 | tf_op jit(solution)/shard_map/all_gather | solution.py:29
  183.3 213.5 %all-gather.6.cloned.1.call-start = ((), (), s32[]{:S(2)}) async-start(), calls=%async_computation.3 | async-start | bytes 4456448 | tf_op jit(solution)/shard_map/all_gather | solution.py:79
  183.9 285.4 %all-gather.8.cloned.1.call-start = ((), (), s32[]{:S(2)}) async-start(), calls=%async_computation.6 | async-start | bytes 4456448 | tf_op jit(solution)/shard_map/all_gather | solution.py:96
  245.4 428.9 %reduce-scatter.3.cloned.1.call-start = ((), (), s32[]{:S(2)}) async-start(), calls=%async_computation.4 | async-start | bytes 2228224 | tf_op jit(solution)/shard_map/reduce_scatter | solution.py:98
  395.2 1.6 copy-start.4
  395.2 1.6 copy-start.6
  404.2 270.1 %copy-start.1 = (bf16[1024,512]{1,0:T(8,128)(2,1)S(1)}, bf16[1024,512]{1,0:T(8,128)(2,1)}, u32[]{:S(2)}) copy-start(bf16[1024,512]{1,0:T(8,128)(2,1)} %param.19) | copy-start | bytes 3145732
Sparse Core Ops, SparseCore 0:
  12.9 159.5 all-reduce.2
  182.7 62.6 reduce-scatter.4
  248.8 78.1 all-gather.3
  328.9 35.9 all-gather.5
  367.6 101.6 all-gather.7
  473.5 200.7 reduce-scatter.2
